TPU v7x, 512 devices: a whole 4x8x8 slice. The times are simulated.
512 devices in a mesh: alpha: 16 (over x, z_hi), beta: 32 (over z_lo, y, core).
Axes of the slice: x: 4, y: 8, z: 8 (z_hi: 4, z_lo: 2; z = z_hi * 2 + z_lo), core: 2. Of those that a mesh axis runs over, the one named last changes fastest.
Arguments:
- amplitudes: float32 [12288, 12288], P('alpha', 'beta'), may hold values from -6 to 6
- coupled_index: int32 [96, 16], P('beta'), may hold values from 0 to 95, as said below
- coupling_blocks: bfloat16 [96, 16, 128, 128], P('beta'), may hold values from -0.125 to 0.125
- string_energy: float32 [12288], replicated, may hold values from -1 to 1
- shift_index: int32 [2], replicated, may hold values from 0 to 12287
Outputs:
- refined: float32 [12288, 12288], P('alpha', 'beta')
Inputs may be any that keep to these rules, and one draw needn't show every extreme that they name: `coupled_index`: row J holds 16 different blocks, each (J + d) mod 96 for some d with |d| <= 9.
All inputs are finite; a program needn't handle non-finite values.
Results may differ from a plain program's by a relative error of at most 0.0035.
Values may be sent and summed in bfloat16 or wider, within the bound.
A program may use at most 64 MiB of HBM per device.

v0:
```python
import jax
import jax.numpy as jnp
from jax import lax
from jax.sharding import PartitionSpec as P

BLK_DEV = 3
REACH = 9
STEPS = 2
HOPS = 3


def shifted(value, axis, by):
    size = lax.axis_size(axis)
    return lax.ppermute(value, axis, [(i, (i + by) % size) for i in range(size)])


def neighbour_tiles(rounded):
    tiles = {0: rounded}
    for direction in (1, -1):
        for distance in range(1, HOPS + 1):
            tiles[-direction * distance] = shifted(rounded, "beta", direction * distance)
    return tiles


def mirrored_tile(local_tile):
    row_count, col_count = local_tile.shape
    alpha_count = lax.axis_size("alpha")
    folded = row_count // col_count
    pieces = local_tile.reshape(folded, alpha_count, col_count // alpha_count, col_count)
    pieces = lax.all_to_all(
        lax.all_to_all(pieces, "alpha", split_axis=1, concat_axis=0, tiled=True),
        "beta",
        split_axis=0,
        concat_axis=1,
        tiled=True,
    )
    pieces = lax.all_to_all(pieces, "alpha", split_axis=1, concat_axis=2, tiled=True)
    squares = pieces.reshape(folded, col_count, col_count)
    return jnp.swapaxes(squares, 1, 2).reshape(row_count, col_count)


def local(amplitudes, coupled_index, coupling_blocks, string_energy, shift_index):
    row_count, col_count = amplitudes.shape
    block_total = BLK_DEV * lax.axis_size("beta")
    band_blocks = (2 * HOPS + 1) * BLK_DEV
    beta_place = lax.axis_index("beta")
    alpha_place = lax.axis_index("alpha")
    local_block = jnp.arange(BLK_DEV, dtype=jnp.int32)
    global_block = beta_place * BLK_DEV + local_block
    offset = (coupled_index - global_block[:, None] + REACH) % block_total - REACH
    position = HOPS * BLK_DEV + local_block[:, None] + offset
    select = (
        position[None, :, :] == jnp.arange(band_blocks, dtype=jnp.int32)[:, None, None]
    ).astype(jnp.bfloat16)
    banded = jnp.einsum(
        "pjs,jsxy->pxjy", select, coupling_blocks, preferred_element_type=jnp.float32
    )
    banded = banded.astype(jnp.bfloat16).reshape(2 * HOPS + 1, col_count, col_count)
    row_energy = lax.dynamic_slice_in_dim(string_energy, alpha_place * row_count, row_count)
    col_energy = lax.dynamic_slice_in_dim(string_energy, beta_place * col_count, col_count)
    diagonal_sum = row_energy[:, None] + col_energy[None, :]
    positions = jnp.arange(string_energy.shape[0], dtype=jnp.int32)
    current = amplitudes
    for iteration in range(STEPS):
        rounded = current.astype(jnp.bfloat16)
        tiles = neighbour_tiles(rounded)
        mixed = jnp.zeros((row_count, col_count), jnp.float32)
        for distance in range(-HOPS, HOPS + 1):
            mixed = mixed + jnp.dot(
                tiles[distance], banded[distance + HOPS], preferred_element_type=jnp.float32
            )
        mixed_low = mixed.astype(jnp.bfloat16)
        mirror = mirrored_tile(mixed_low)
        sigma = mixed_low.astype(jnp.float32) + mirror.astype(jnp.float32)
        shift = 2.0 * jnp.sum(jnp.where(positions == shift_index[iteration], string_energy, 0.0))
        residual = sigma - shift * current
        gap = diagonal_sum - shift
        current = current - residual * gap / (gap * gap + 1.0)
    return current


def solution(mesh):
    placed = (P("alpha", "beta"), P("beta", None), P("beta", None, None, None), P(), P())
    return jax.shard_map(
        local, mesh=mesh, in_specs=placed, out_specs=P("alpha", "beta"), check_vma=False
    )
```

profile of v0, /device:TPU:8, one launch (start us, length us, event | category | flops | bytes accessed | tf_op | source)
XLA Modules:
  0.0 263.7 jit_solution(12224040533477362843)
XLA Ops:
  1.5 1.9 collective-permute-start.2
  3.4 3.5 %collective-permute-start.1 = (bf16[768,384]{1,0:T(8,128)(2,1)S(1)}, bf16[768,384]{1,0:T(8,128)(2,1)S(1)}, u32[]{:S(2)}, u32[]{:S(2)}) collective-permute-start(bf16[768,384]{1,0:T(8,128)(2,1)S(1)} %convert_element_type.57), channel_id=1, source_target_pairs={{0,2},{1,3},{2,4},{3,5},{4,6},{5,7},{6,8},{7,9},{8,10},{9,11},{10,... | collective-permute-start | bytes 1769480 | tf_op jit(solution)/shard_map/ppermute | solution.py:14
  6.9 5.7 %collective-permute-start = (bf16[768,384]{1,0:T(8,128)(2,1)S(1)}, bf16[768,384]{1,0:T(8,128)(2,1)S(1)}, u32[]{:S(2)}, u32[]{:S(2)}) collective-permute-start(bf16[768,384]{1,0:T(8,128)(2,1)S(1)} %convert_element_type.57), channel_id=1, source_target_pairs={{0,3},{1,4},{2,5},{3,6},{4,7},{5,8},{6,9},{7,10},{8,11},{9,12},{10... | collective-permute-start | bytes 1769480 | tf_op jit(solution)/shard_map/ppermute | solution.py:14
  12.6 5.7 %collective-permute-start.5 = (bf16[768,384]{1,0:T(8,128)(2,1)S(1)}, bf16[768,384]{1,0:T(8,128)(2,1)}, u32[]{:S(2)}, u32[]{:S(2)}) collective-permute-start(bf16[768,384]{1,0:T(8,128)(2,1)S(1)} %convert_element_type.57), channel_id=1, source_target_pairs={{0,29},{1,30},{2,31},{3,0},{4,1},{5,2},{6,3},{7,4},{8,5},{9,6},{10... | collective-permute-start | bytes 1769480 | tf_op jit(solution)/shard_map/ppermute | solution.py:14
  18.3 3.6 %collective-permute-start.4 = (bf16[768,384]{1,0:T(8,128)(2,1)S(1)}, bf16[768,384]{1,0:T(8,128)(2,1)}, u32[]{:S(2)}, u32[]{:S(2)}) collective-permute-start(bf16[768,384]{1,0:T(8,128)(2,1)S(1)} %convert_element_type.57), channel_id=1, source_target_pairs={{0,30},{1,31},{2,0},{3,1},{4,2},{5,3},{6,4},{7,5},{8,6},{9,7},{10,... | collective-permute-start | bytes 1769480 | tf_op jit(solution)/shard_map/ppermute | solution.py:14
  23.4 1.5 fusion.67
  27.7 2.2 collective-permute-start.3
  29.9 1.6 fusion.38
  32.0 4.6 %collective-permute-done.5 = bf16[768,384]{1,0:T(8,128)(2,1)} collective-permute-done((bf16[768,384]{1,0:T(8,128)(2,1)S(1)}, bf16[768,384]{1,0:T(8,128)(2,1)}, u32[]{:S(2)}, u32[]{:S(2)}) %collective-permute-start.5) | collective-permute-done | bytes 589856 | tf_op jit(solution)/shard_map/ppermute | solution.py:14
  36.6 1.6 fusion.24
  38.1 9.6 %collective-permute-done.4 = bf16[768,384]{1,0:T(8,128)(2,1)} collective-permute-done((bf16[768,384]{1,0:T(8,128)(2,1)S(1)}, bf16[768,384]{1,0:T(8,128)(2,1)}, u32[]{:S(2)}, u32[]{:S(2)}) %collective-permute-start.4) | collective-permute-done | bytes 589856 | tf_op jit(solution)/shard_map/ppermute | solution.py:14
  47.7 1.6 fusion.28
  49.3 2.4 collective-permute-done
  54.3 33.0 %all_to_all.84 = bf16[2,16,24,384]{3,2,0,1:T(8,128)(2,1)S(1)} all-to-all(bf16[2,16,24,384]{3,2,0,1:T(8,128)(2,1)S(1)} %copy.74), channel_id=1, replica_groups=mesh['alpha'=16,'beta'=32] {'alpha'}, dimensions={1} | all-to-all | bytes 1179648 | tf_op jit(solution)/shard_map/all_to_all | solution.py:31
  87.3 25.6 %all_to_all.85 = bf16[32,1,24,384]{3,2,1,0:T(8,128)(2,1)} all-to-all(bf16[32,1,24,384]{3,2,1,0:T(8,128)(2,1)S(1)} %bitcast.138), channel_id=1, replica_groups=mesh['alpha'=16,'beta'=32] {'beta'}, dimensions={0} | all-to-all | bytes 1179648 | tf_op jit(solution)/shard_map/all_to_all | solution.py:30
  112.9 4.3 %all-to-all-start.2 = ((bf16[1,32,24,384]{3,2,0,1:T(8,128)(2,1)}), bf16[1,32,24,384]{3,2,0,1:T(8,128)(2,1)}, u32[]{:S(2)}, u32[]{:S(2)}) async-start(bf16[1,32,24,384]{3,2,0,1:T(8,128)(2,1)} %bitcast.137), calls=%async_computation.2 | async-start | bytes 1179648 | tf_op jit(solution)/shard_map/all_to_all | solution.py:37
  119.3 1.9 select_reduce_fusion
  121.8 14.8 %all-to-all-done.2 = bf16[1,32,24,384]{3,2,0,1:T(8,128)(2,1)} async-done(((bf16[1,32,24,384]{3,2,0,1:T(8,128)(2,1)}), bf16[1,32,24,384]{3,2,0,1:T(8,128)(2,1)}, u32[]{:S(2)}, u32[]{:S(2)}) %all-to-all-start.2) | async-done | bytes 589856 | tf_op jit(solution)/shard_map/all_to_all | solution.py:37
  139.2 1.6 fusion.65
  140.7 2.5 collective-permute-start.7
  143.2 1.9 collective-permute-start.8
  145.2 3.6 %collective-permute-start.10 = (bf16[768,384]{0,1:T(8,128)(2,1)S(1)}, bf16[768,384]{0,1:T(8,128)(2,1)S(1)}, u32[]{:S(2)}, u32[]{:S(2)}) collective-permute-start(bf16[768,384]{0,1:T(8,128)(2,1)S(1)} %get-tuple-element.7), channel_id=1, source_target_pairs={{0,30},{1,31},{2,0},{3,1},{4,2},{5,3},{6,4},{7,5},{8,6},{9,7},{10,... | collective-permute-start | bytes 1769480 | tf_op jit(solution)/shard_map/ppermute | solution.py:14
  149.3 3.1 %collective-permute-start.6 = (bf16[768,384]{0,1:T(8,128)(2,1)S(1)}, bf16[768,384]{0,1:T(8,128)(2,1)S(1)}, u32[]{:S(2)}, u32[]{:S(2)}) collective-permute-start(bf16[768,384]{0,1:T(8,128)(2,1)S(1)} %get-tuple-element.7), channel_id=1, source_target_pairs={{0,3},{1,4},{2,5},{3,6},{4,7},{5,8},{6,9},{7,10},{8,11},{9,12},{10... | collective-permute-start | bytes 1769480 | tf_op jit(solution)/shard_map/ppermute | solution.py:14
  152.4 5.6 %collective-permute-start.11 = (bf16[768,384]{0,1:T(8,128)(2,1)S(1)}, bf16[768,384]{0,1:T(8,128)(2,1)S(1)}, u32[]{:S(2)}, u32[]{:S(2)}) collective-permute-start(bf16[768,384]{0,1:T(8,128)(2,1)S(1)} %get-tuple-element.7), channel_id=1, source_target_pairs={{0,29},{1,30},{2,31},{3,0},{4,1},{5,2},{6,3},{7,4},{8,5},{9,6},{10... | collective-permute-start | bytes 1769480 | tf_op jit(solution)/shard_map/ppermute | solution.py:14
  159.0 3.7 %collective-permute-start.9 = (bf16[768,384]{0,1:T(8,128)(2,1)S(1)}, bf16[768,384]{0,1:T(8,128)(2,1)S(1)}, u32[]{:S(2)}, u32[]{:S(2)}) collective-permute-start(bf16[768,384]{0,1:T(8,128)(2,1)S(1)} %get-tuple-element.7), channel_id=1, source_target_pairs={{0,31},{1,0},{2,1},{3,2},{4,3},{5,4},{6,5},{7,6},{8,7},{9,8},{10,9... | collective-permute-start | bytes 1769480 | tf_op jit(solution)/shard_map/ppermute | solution.py:14
  163.2 4.1 %collective-permute-done.8 = bf16[768,384]{0,1:T(8,128)(2,1)S(1)} collective-permute-done((bf16[768,384]{0,1:T(8,128)(2,1)S(1)}, bf16[768,384]{0,1:T(8,128)(2,1)S(1)}, u32[]{:S(2)}, u32[]{:S(2)}) %collective-permute-start.8) | collective-permute-done | bytes 589856 | tf_op jit(solution)/shard_map/ppermute | solution.py:14
  168.4 14.0 %collective-permute-done.11 = bf16[768,384]{0,1:T(8,128)(2,1)S(1)} collective-permute-done((bf16[768,384]{0,1:T(8,128)(2,1)S(1)}, bf16[768,384]{0,1:T(8,128)(2,1)S(1)}, u32[]{:S(2)}, u32[]{:S(2)}) %collective-permute-start.11) | collective-permute-done | bytes 589856 | tf_op jit(solution)/shard_map/ppermute | solution.py:14
  183.6 3.6 %collective-permute-done.9 = bf16[768,384]{0,1:T(8,128)(2,1)S(1)} collective-permute-done((bf16[768,384]{0,1:T(8,128)(2,1)S(1)}, bf16[768,384]{0,1:T(8,128)(2,1)S(1)}, u32[]{:S(2)}, u32[]{:S(2)}) %collective-permute-start.9) | collective-permute-done | bytes 589856 | tf_op jit(solution)/shard_map/ppermute | solution.py:14
  188.2 24.6 %all_to_all.86 = bf16[2,16,24,384]{3,2,0,1:T(8,128)(2,1)S(1)} all-to-all(bf16[2,16,24,384]{3,2,0,1:T(8,128)(2,1)S(1)} %copy.90), channel_id=1, replica_groups=mesh['alpha'=16,'beta'=32] {'alpha'}, dimensions={1} | all-to-all | bytes 1179648 | tf_op jit(solution)/shard_map/all_to_all | solution.py:31
  212.8 24.5 %all_to_all.87 = bf16[32,1,24,384]{3,2,1,0:T(8,128)(2,1)} all-to-all(bf16[32,1,24,384]{3,2,1,0:T(8,128)(2,1)S(1)} %bitcast.139), channel_id=1, replica_groups=mesh['alpha'=16,'beta'=32] {'beta'}, dimensions={0} | all-to-all | bytes 1179648 | tf_op jit(solution)/shard_map/all_to_all | solution.py:30
  237.3 3.6 %all-to-all-start.5 = ((bf16[1,32,24,384]{3,2,0,1:T(8,128)(2,1)}), bf16[1,32,24,384]{3,2,0,1:T(8,128)(2,1)S(1)}, u32[]{:S(2)}, u32[]{:S(2)}) async-start(bf16[1,32,24,384]{3,2,0,1:T(8,128)(2,1)} %bitcast.23), calls=%async_computation.5 | async-start | bytes 1179648 | tf_op jit(solution)/shard_map/all_to_all | solution.py:37
  241.5 18.8 %all-to-all-done.5 = bf16[1,32,24,384]{3,2,0,1:T(8,128)(2,1)S(1)} async-done(((bf16[1,32,24,384]{3,2,0,1:T(8,128)(2,1)}), bf16[1,32,24,384]{3,2,0,1:T(8,128)(2,1)S(1)}, u32[]{:S(2)}, u32[]{:S(2)}) %all-to-all-start.5) | async-done | bytes 589856 | tf_op jit(solution)/shard_map/all_to_all | solution.py:37
  (86 shorter events, 21.7 us)
Async XLA Ops:
  0.0 22.0 %copy-start = (bf16[3,16,128,128]{3,2,1,0:T(8,128)(2,1)S(1)}, bf16[3,16,128,128]{3,2,1,0:T(8,128)(2,1)}, u32[]{:S(2)}) copy-start(bf16[3,16,128,128]{3,2,1,0:T(8,128)(2,1)} %param.7) | copy-start | bytes 4718596
  0.0 22.0 %copy-start.19 = (s32[3,16]{1,0:T(4,128)S(1)}, s32[3,16]{1,0:T(4,128)}, u32[]{:S(2)}) copy-start(s32[3,16]{1,0:T(4,128)} %param.6) | copy-start | bytes 580
  1.5 26.2 %collective-permute-start.2 = (bf16[768,384]{1,0:T(8,128)(2,1)S(1)}, bf16[768,384]{1,0:T(8,128)(2,1)}, u32[]{:S(2)}, u32[]{:S(2)}) collective-permute-start(bf16[768,384]{1,0:T(8,128)(2,1)S(1)} %convert_element_type.57), channel_id=1, source_target_pairs={{0,1},{1,2},{2,3},{3,4},{4,5},{5,6},{6,7},{7,8},{8,9},{9,10},{10,1... | collective-permute-start | bytes 1769480 | tf_op jit(solution)/shard_map/ppermute | solution.py:14
  3.4 28.0 %collective-permute-start.1 = (bf16[768,384]{1,0:T(8,128)(2,1)S(1)}, bf16[768,384]{1,0:T(8,128)(2,1)S(1)}, u32[]{:S(2)}, u32[]{:S(2)}) collective-permute-start(bf16[768,384]{1,0:T(8,128)(2,1)S(1)} %convert_element_type.57), channel_id=1, source_target_pairs={{0,2},{1,3},{2,4},{3,5},{4,6},{5,7},{6,8},{7,9},{8,10},{9,11},{10,... | collective-permute-start | bytes 1769480 | tf_op jit(solution)/shard_map/ppermute | solution.py:14
  6.9 44.8 %collective-permute-start = (bf16[768,384]{1,0:T(8,128)(2,1)S(1)}, bf16[768,384]{1,0:T(8,128)(2,1)S(1)}, u32[]{:S(2)}, u32[]{:S(2)}) collective-permute-start(bf16[768,384]{1,0:T(8,128)(2,1)S(1)} %convert_element_type.57), channel_id=1, source_target_pairs={{0,3},{1,4},{2,5},{3,6},{4,7},{5,8},{6,9},{7,10},{8,11},{9,12},{10... | collective-permute-start | bytes 1769480 | tf_op jit(solution)/shard_map/ppermute | solution.py:14
  12.6 24.0 %collective-permute-start.5 = (bf16[768,384]{1,0:T(8,128)(2,1)S(1)}, bf16[768,384]{1,0:T(8,128)(2,1)}, u32[]{:S(2)}, u32[]{:S(2)}) collective-permute-start(bf16[768,384]{1,0:T(8,128)(2,1)S(1)} %convert_element_type.57), channel_id=1, source_target_pairs={{0,29},{1,30},{2,31},{3,0},{4,1},{5,2},{6,3},{7,4},{8,5},{9,6},{10... | collective-permute-start | bytes 1769480 | tf_op jit(solution)/shard_map/ppermute | solution.py:14
  18.3 29.4 %collective-permute-start.4 = (bf16[768,384]{1,0:T(8,128)(2,1)S(1)}, bf16[768,384]{1,0:T(8,128)(2,1)}, u32[]{:S(2)}, u32[]{:S(2)}) collective-permute-start(bf16[768,384]{1,0:T(8,128)(2,1)S(1)} %convert_element_type.57), channel_id=1, source_target_pairs={{0,30},{1,31},{2,0},{3,1},{4,2},{5,3},{6,4},{7,5},{8,6},{9,7},{10,... | collective-permute-start | bytes 1769480 | tf_op jit(solution)/shard_map/ppermute | solution.py:14
  26.0 3.8 %copy-start.10 = (bf16[3,128,3,128]{3,2,1,0:T(4,128)(2,1)}, bf16[3,128,3,128]{3,2,1,0:T(4,128)(2,1)S(1)}, u32[]{:S(2)}) copy-start(bf16[3,128,3,128]{3,2,1,0:T(4,128)(2,1)S(1)} %copy.68) | copy-start | bytes 884740
  26.4 5.1 %copy-start.14 = (bf16[3,128,3,128]{3,2,1,0:T(4,128)(2,1)}, bf16[3,128,3,128]{3,2,1,0:T(4,128)(2,1)S(1)}, u32[]{:S(2)}) copy-start(bf16[3,128,3,128]{3,2,1,0:T(4,128)(2,1)S(1)} %copy.67) | copy-start | bytes 884740
  26.7 25.0 %copy-start.6 = (bf16[3,128,3,128]{3,2,1,0:T(4,128)(2,1)}, bf16[3,128,3,128]{3,2,1,0:T(4,128)(2,1)S(1)}, u32[]{:S(2)}) copy-start(bf16[3,128,3,128]{3,2,1,0:T(4,128)(2,1)S(1)} %copy.66) | copy-start | bytes 884740
  27.0 9.6 %copy-start.8 = (bf16[3,128,3,128]{3,2,1,0:T(4,128)(2,1)}, bf16[3,128,3,128]{3,2,1,0:T(4,128)(2,1)S(1)}, u32[]{:S(2)}) copy-start(bf16[3,128,3,128]{3,2,1,0:T(4,128)(2,1)S(1)} %copy.72) | copy-start | bytes 884740
  27.3 20.4 %copy-start.12 = (bf16[3,128,3,128]{3,2,1,0:T(4,128)(2,1)}, bf16[3,128,3,128]{3,2,1,0:T(4,128)(2,1)S(1)}, u32[]{:S(2)}) copy-start(bf16[3,128,3,128]{3,2,1,0:T(4,128)(2,1)S(1)} %copy.71) | copy-start | bytes 884740
  27.6 25.8 %copy-start.4 = (bf16[3,128,3,128]{3,2,1,0:T(4,128)(2,1)}, bf16[3,128,3,128]{3,2,1,0:T(4,128)(2,1)S(1)}, u32[]{:S(2)}) copy-start(bf16[3,128,3,128]{3,2,1,0:T(4,128)(2,1)S(1)} %copy.70) | copy-start | bytes 884740
  27.7 25.7 %collective-permute-start.3 = (bf16[768,384]{1,0:T(8,128)(2,1)S(1)}, bf16[768,384]{1,0:T(8,128)(2,1)S(1)}, u32[]{:S(2)}, u32[]{:S(2)}) collective-permute-start(bf16[768,384]{1,0:T(8,128)(2,1)S(1)} %convert_element_type.57), channel_id=1, source_target_pairs={{0,31},{1,0},{2,1},{3,2},{4,3},{5,4},{6,5},{7,6},{8,7},{9,8},{10,9... | collective-permute-start | bytes 1769480 | tf_op jit(solution)/shard_map/ppermute | solution.py:14
  87.3 29.9 %copy-start.1 = (f32[768,384]{1,0:T(8,128)S(1)}, f32[768,384]{1,0:T(8,128)}, u32[]{:S(2)}) copy-start(f32[768,384]{1,0:T(8,128)} %param.5) | copy-start | bytes 3538948
  112.9 23.7 %all-to-all-start.2 = ((bf16[1,32,24,384]{3,2,0,1:T(8,128)(2,1)}), bf16[1,32,24,384]{3,2,0,1:T(8,128)(2,1)}, u32[]{:S(2)}, u32[]{:S(2)}) async-start(bf16[1,32,24,384]{3,2,0,1:T(8,128)(2,1)} %bitcast.137), calls=%async_computation.2 | async-start | bytes 1179648 | tf_op jit(solution)/shard_map/all_to_all | solution.py:37
  117.2 1.4 copy-start.18
  117.2 1.6 copy-start.20
  139.1 9.6 %copy-start.17 = (bf16[3,128,3,128]{3,2,1,0:T(4,128)(2,1)S(1)}, bf16[3,128,3,128]{3,2,1,0:T(4,128)(2,1)}, u32[]{:S(2)}) copy-start(bf16[3,128,3,128]{3,2,1,0:T(4,128)(2,1)} %copy-done.16) | copy-start | bytes 884740
  140.7 21.9 %copy-start.15 = (bf16[3,128,3,128]{3,2,1,0:T(4,128)(2,1)S(1)}, bf16[3,128,3,128]{3,2,1,0:T(4,128)(2,1)}, u32[]{:S(2)}) copy-start(bf16[3,128,3,128]{3,2,1,0:T(4,128)(2,1)} %copy-done.14) | copy-start | bytes 884740
  140.7 18.3 %collective-permute-start.7 = (bf16[768,384]{0,1:T(8,128)(2,1)S(1)}, bf16[768,384]{0,1:T(8,128)(2,1)S(1)}, u32[]{:S(2)}, u32[]{:S(2)}) collective-permute-start(bf16[768,384]{0,1:T(8,128)(2,1)S(1)} %get-tuple-element.7), channel_id=1, source_target_pairs={{0,2},{1,3},{2,4},{3,5},{4,6},{5,7},{6,8},{7,9},{8,10},{9,11},{10,... | collective-permute-start | bytes 1769480 | tf_op jit(solution)/shard_map/ppermute | solution.py:14
  143.2 24.1 %collective-permute-start.8 = (bf16[768,384]{0,1:T(8,128)(2,1)S(1)}, bf16[768,384]{0,1:T(8,128)(2,1)S(1)}, u32[]{:S(2)}, u32[]{:S(2)}) collective-permute-start(bf16[768,384]{0,1:T(8,128)(2,1)S(1)} %get-tuple-element.7), channel_id=1, source_target_pairs={{0,1},{1,2},{2,3},{3,4},{4,5},{5,6},{6,7},{7,8},{8,9},{9,10},{10,1... | collective-permute-start | bytes 1769480 | tf_op jit(solution)/shard_map/ppermute | solution.py:14
  145.2 22.7 %collective-permute-start.10 = (bf16[768,384]{0,1:T(8,128)(2,1)S(1)}, bf16[768,384]{0,1:T(8,128)(2,1)S(1)}, u32[]{:S(2)}, u32[]{:S(2)}) collective-permute-start(bf16[768,384]{0,1:T(8,128)(2,1)S(1)} %get-tuple-element.7), channel_id=1, source_target_pairs={{0,30},{1,31},{2,0},{3,1},{4,2},{5,3},{6,4},{7,5},{8,6},{9,7},{10,... | collective-permute-start | bytes 1769480 | tf_op jit(solution)/shard_map/ppermute | solution.py:14
  149.3 18.0 %copy-start.11 = (bf16[3,128,3,128]{3,2,1,0:T(4,128)(2,1)S(1)}, bf16[3,128,3,128]{3,2,1,0:T(4,128)(2,1)}, u32[]{:S(2)}) copy-start(bf16[3,128,3,128]{3,2,1,0:T(4,128)(2,1)} %copy-done.10) | copy-start | bytes 884740
  149.3 33.8 %collective-permute-start.6 = (bf16[768,384]{0,1:T(8,128)(2,1)S(1)}, bf16[768,384]{0,1:T(8,128)(2,1)S(1)}, u32[]{:S(2)}, u32[]{:S(2)}) collective-permute-start(bf16[768,384]{0,1:T(8,128)(2,1)S(1)} %get-tuple-element.7), channel_id=1, source_target_pairs={{0,3},{1,4},{2,5},{3,6},{4,7},{5,8},{6,9},{7,10},{8,11},{9,12},{10... | collective-permute-start | bytes 1769480 | tf_op jit(solution)/shard_map/ppermute | solution.py:14
  152.4 30.0 %collective-permute-start.11 = (bf16[768,384]{0,1:T(8,128)(2,1)S(1)}, bf16[768,384]{0,1:T(8,128)(2,1)S(1)}, u32[]{:S(2)}, u32[]{:S(2)}) collective-permute-start(bf16[768,384]{0,1:T(8,128)(2,1)S(1)} %get-tuple-element.7), channel_id=1, source_target_pairs={{0,29},{1,30},{2,31},{3,0},{4,1},{5,2},{6,3},{7,4},{8,5},{9,6},{10... | collective-permute-start | bytes 1769480 | tf_op jit(solution)/shard_map/ppermute | solution.py:14
  159.0 28.2 %collective-permute-start.9 = (bf16[768,384]{0,1:T(8,128)(2,1)S(1)}, bf16[768,384]{0,1:T(8,128)(2,1)S(1)}, u32[]{:S(2)}, u32[]{:S(2)}) collective-permute-start(bf16[768,384]{0,1:T(8,128)(2,1)S(1)} %get-tuple-element.7), channel_id=1, source_target_pairs={{0,31},{1,0},{2,1},{3,2},{4,3},{5,4},{6,5},{7,6},{8,7},{9,8},{10,9... | collective-permute-start | bytes 1769480 | tf_op jit(solution)/shard_map/ppermute | solution.py:14
  163.2 4.7 %copy-start.13 = (bf16[3,128,3,128]{3,2,1,0:T(4,128)(2,1)S(1)}, bf16[3,128,3,128]{3,2,1,0:T(4,128)(2,1)}, u32[]{:S(2)}) copy-start(bf16[3,128,3,128]{3,2,1,0:T(4,128)(2,1)} %copy-done.12) | copy-start | bytes 884740
  167.9 14.6 %copy-start.9 = (bf16[3,128,3,128]{3,2,1,0:T(4,128)(2,1)S(1)}, bf16[3,128,3,128]{3,2,1,0:T(4,128)(2,1)}, u32[]{:S(2)}) copy-start(bf16[3,128,3,128]{3,2,1,0:T(4,128)(2,1)} %copy-done.8) | copy-start | bytes 884740
  168.4 14.7 %copy-start.7 = (bf16[3,128,3,128]{3,2,1,0:T(4,128)(2,1)S(1)}, bf16[3,128,3,128]{3,2,1,0:T(4,128)(2,1)}, u32[]{:S(2)}) copy-start(bf16[3,128,3,128]{3,2,1,0:T(4,128)(2,1)} %copy-done.6) | copy-start | bytes 884740
  183.0 4.3 %copy-start.5 = (bf16[3,128,3,128]{3,2,1,0:T(4,128)(2,1)S(1)}, bf16[3,128,3,128]{3,2,1,0:T(4,128)(2,1)}, u32[]{:S(2)}) copy-start(bf16[3,128,3,128]{3,2,1,0:T(4,128)(2,1)} %copy-done.4) | copy-start | bytes 884740
  237.3 23.0 %all-to-all-start.5 = ((bf16[1,32,24,384]{3,2,0,1:T(8,128)(2,1)}), bf16[1,32,24,384]{3,2,0,1:T(8,128)(2,1)S(1)}, u32[]{:S(2)}, u32[]{:S(2)}) async-start(bf16[1,32,24,384]{3,2,0,1:T(8,128)(2,1)} %bitcast.23), calls=%async_computation.5 | async-start | bytes 1179648 | tf_op jit(solution)/shard_map/all_to_all | solution.py:37
  (3 other events, 3.4 us)
where the time goes:
time: 265 us; the launch traced here: 264 us
  blocking collectives  108 us (41%)
  waiting for transfers between devices  74.2 us (28%)
  starting transfers between devices  50.9 us (19%)
  matrix products  11.7 us (4%)
  local copies, waits for them, and re-layouts  10.7 us (4%)
  other arithmetic  6.75 us (3%)
    all_to_all x2, blocking collectives, mirrored_tile(): lax.all_to_all(pieces, 'alpha', split_axis=1, concat_axis=0, tiled=True)  57.5 us
    all_to_all x2, blocking collectives, mirrored_tile(): lax.all_to_all(lax.all_to_all(pieces, 'alpha', split_axis=1, concat_axis=...  50.2 us
    ppermute x12, starting transfers between devices, shifted(): lax.ppermute(value, axis, [(i, (i + by) % size) for i in range(size)])  43 us
    ppermute x12, waiting for transfers between devices, shifted(): lax.ppermute(value, axis, [(i, (i + by) % size) for i in range(size)])  40.6 us
    all_to_all x2, waiting for transfers between devices, mirrored_tile(): lax.all_to_all(pieces, 'alpha', split_axis=1, concat_axis=2, tiled=True)  33.6 us
    dot_general x14, matrix products, local(): jnp.dot(tiles[distance], banded[distance + HOPS], preferred_element_type=...  10.4 us
    all_to_all x2, starting transfers between devices, mirrored_tile(): lax.all_to_all(pieces, 'alpha', split_axis=1, concat_axis=2, tiled=True)  7.84 us
  transfers between devices with their start and end apart: 14, of which 11 were waited for; matrix products, arithmetic and copies ran while one was open for 7% of the time, Pallas kernels for 0%

commit v1 on v0

v1 whole, which is shorter than its diff:
```python
import functools

import jax
import jax.numpy as jnp
from jax import lax
from jax.experimental import pallas as pl
from jax.experimental.pallas import tpu as pltpu
from jax.sharding import PartitionSpec as P

BLK = 128
REACH = 9
STEPS = 2
HOPS = 3
TILES = 2 * HOPS + 1
CHUNKS = 6
SPREAD = 8
MESH = pl.DeviceIdType.MESH


def kernel(
    amp_hbm, idx_ref, coup_hbm, energy_ref, shift_ref, out_ref,
    cur, halo, coup, banded, weight, mixed, inter, fin, pos_ref,
    load_sem, coup_sem, hsend, hrecv, leg1_send, leg1_recv, leg2_send, leg2_recv,
):
    rows, cols = amp_hbm.shape
    chunk_rows = rows // CHUNKS
    half = rows // 2
    piece = half // SPREAD
    blocks = cols // BLK
    couple = coup_hbm.shape[1]
    alpha = lax.axis_index("alpha")
    beta = lax.axis_index("beta")
    chip = beta // 2
    core = beta % 2
    chips = lax.axis_size("beta") // 2
    right = 2 * ((chip + 1) % chips)
    left = 2 * ((chip + chips - 1) % chips)
    sibling = 2 * chip + 1 - core
    far = 2 * ((chip + chips + 2 * core - 1) % chips) + 1 - core
    beta_group = beta // (2 * SPREAD)
    own_place = chip % SPREAD

    def load(i):
        at = pl.ds(i * chunk_rows, chunk_rows)
        return pltpu.make_async_copy(amp_hbm.at[at], cur.at[at], load_sem.at[i])

    def coup_copy():
        return pltpu.make_async_copy(coup_hbm, coup.at[pl.ds(0, blocks)], coup_sem)

    for i in range(CHUNKS):
        load(i).start()
    coup_copy().start()

    def remote(step, kind, i, src_slot, dst_slot, to):
        at = pl.ds(pl.multiple_of(i * chunk_rows, chunk_rows), chunk_rows)
        return pltpu.make_async_remote_copy(
            halo.at[step, src_slot, at],
            halo.at[step, dst_slot, at],
            hsend.at[step, kind, i],
            hrecv.at[step, kind, i],
            device_id=(alpha, to),
            device_id_type=MESH,
        )

    def to_right(step, i):
        return remote(step, 0, i, 3, 1, right + core)

    def to_left(step, i):
        return remote(step, 1, i, 3, 5, left + core)

    def to_sibling(step, i):
        return remote(step, 2, i, 3, 2 * core + 2, sibling)

    def pass_left_tile(step, i):
        return remote(step, 3, i, 1, 2 * core, sibling)

    def pass_right_tile(step, i):
        return remote(step, 4, i, 5, 2 * core + 4, sibling)

    def pass_far(step, i):
        return remote(step, 5, i, 5 - 4 * core, 6 - 6 * core, far)

    halo_kinds = (to_right, to_left, to_sibling, pass_left_tile, pass_right_tile, pass_far)

    def start_own(step, i):
        to_right(step, i).start()
        to_left(step, i).start()
        to_sibling(step, i).start()

    for i in range(CHUNKS):
        load(i).wait()
        at = pl.ds(i * chunk_rows, chunk_rows)
        halo[0, HOPS, at, :] = cur[at, :].astype(jnp.bfloat16)
        start_own(0, i)

    coup_copy().wait()
    coup[blocks, 0] = jnp.zeros((BLK, BLK), jnp.bfloat16)
    total = blocks * lax.axis_size("beta")
    for j in range(blocks):
        mine = beta * blocks + j
        for t in range(couple):
            offset = (idx_ref[j, t] - mine + REACH + total) % total - REACH
            pos_ref[j, t] = HOPS * blocks + j + offset

    def build(slot, carry):
        for u in range(blocks):
            place = slot * blocks + u
            for j in range(blocks):
                found_j = blocks
                found_t = 0
                for t in range(couple):
                    hit = pos_ref[j, t] == place
                    found_j = jnp.where(hit, j, found_j)
                    found_t = jnp.where(hit, t, found_t)
                banded[slot, pl.ds(u * BLK, BLK), pl.ds(j * BLK, BLK)] = coup[found_j, found_t]
        return carry

    lax.fori_loop(0, TILES, build, 0)

    places = lax.broadcasted_iota(jnp.int32, energy_ref.shape, 0) * BLK + lax.broadcasted_iota(
        jnp.int32, energy_ref.shape, 1
    )

    def shift_of(step):
        chosen = jnp.where(places == shift_ref[step], energy_ref[...], 0.0)
        return 2.0 * jnp.sum(chosen)

    row_blocks = rows // BLK

    def fill_weight(step, shift):
        def body(i, carry):
            row_line = energy_ref[pl.ds(alpha * row_blocks + i, 1), :]
            column = jnp.transpose(jnp.broadcast_to(row_line, (BLK, BLK)))
            at = pl.ds(pl.multiple_of(i * BLK, BLK), BLK)
            for j in range(blocks):
                gap = column + energy_ref[pl.ds(beta * blocks + j, 1), :] - shift
                weight[at, pl.ds(j * BLK, BLK)] = gap / (gap * gap + 1.0)
            return carry

        lax.fori_loop(0, row_blocks, body, 0)

    diagonal = (alpha == chip)

    def leg1(step, i):
        place = (own_place + i) % SPREAD
        return pltpu.make_async_remote_copy(
            mixed.at[step, :, i],
            inter.at[step, alpha % SPREAD],
            leg1_send.at[step, i],
            leg1_recv.at[step, alpha % SPREAD],
            device_id=(chip, (alpha // SPREAD) * 2 * SPREAD + 2 * place + core),
            device_id_type=MESH,
        )

    def leg1_self(step):
        return pltpu.make_async_copy(
            mixed.at[step, :, 0],
            inter.at[step, alpha % SPREAD],
            leg1_recv.at[step, alpha % SPREAD],
        )

    source_piece = (own_place + SPREAD - alpha % SPREAD) % SPREAD

    def leg1_arrived(step, m):
        return pltpu.make_async_copy(
            inter.at[step, m], inter.at[step, m], leg1_recv.at[step, m]
        )

    def leg2(step, m, to_core):
        return pltpu.make_async_remote_copy(
            inter.at[step, m, to_core],
            fin.at[step, core, source_piece],
            leg2_send.at[step, m, to_core],
            leg2_recv.at[step, core],
            device_id=(alpha, beta_group * 2 * SPREAD + 2 * m + to_core),
            device_id_type=MESH,
        )

    def leg2_self(step):
        return pltpu.make_async_copy(
            inter.at[step, own_place, core],
            fin.at[step, core, source_piece],
            leg2_recv.at[step, core],
        )

    for step in range(STEPS):
        shift = shift_of(step)
        fill_weight(step, shift)

        def forward(i, carry):
            to_right(step, i).wait_recv()
            pass_left_tile(step, i).start()
            to_left(step, i).wait_recv()
            pass_right_tile(step, i).start()
            pass_far(step, i).start()
            return carry

        lax.fori_loop(0, CHUNKS, forward, 0)

        pieces_per_chunk = chunk_rows // piece if chunk_rows >= piece else 1

        def mix(i, carry):
            for copy in halo_kinds[2:]:
                copy(step, i).wait_recv()
            at = pl.ds(pl.multiple_of(i * chunk_rows, chunk_rows), chunk_rows)
            acc = jnp.dot(halo[step, 0, at, :], banded[0], preferred_element_type=jnp.float32)
            for slot in range(1, TILES):
                acc = acc + jnp.dot(
                    halo[step, slot, at, :], banded[slot], preferred_element_type=jnp.float32
                )
            low = acc.astype(jnp.bfloat16)
            per_half = CHUNKS // 2
            flat = mixed.at[step, i // per_half]
            base = (i % per_half) * chunk_rows
            for q in range(chunk_rows // 16):
                start = base + q * 16
                flat[start // piece, pl.ds(pl.multiple_of(start % piece, 16), 16), :] = low[
                    q * 16 : (q + 1) * 16
                ]
            wide = low.astype(jnp.float32)
            factor = weight[at, :]
            cur[at, :] = cur[at, :] * (1.0 + shift * factor) - wide * factor
            return carry

        lax.fori_loop(0, CHUNKS, mix, 0)

        for i in range(SPREAD):
            if i == 0:
                pl.when(diagonal)(leg1_self(step).start)
                pl.when(jnp.logical_not(diagonal))(leg1(step, i).start)
            else:
                leg1(step, i).start()

        def onward(d, carry):
            m = (own_place + d) % SPREAD
            leg1_arrived(step, m).wait()
            leg2(step, m, 0).start()
            leg2(step, m, 1).start()
            return carry

        lax.fori_loop(1, SPREAD, onward, 0)
        leg1_arrived(step, own_place).wait()
        leg2(step, own_place, 1 - core).start()
        leg2_self(step).start()

        for copy in halo_kinds:
            for i in range(CHUNKS):
                copy(step, i).wait_send()
        for i in range(SPREAD):
            if i == 0:
                pl.when(jnp.logical_not(diagonal))(leg1(step, i).wait_send)
            else:
                leg1(step, i).wait_send()

        per_half = CHUNKS // 2
        for c in range(2):
            pltpu.make_async_copy(fin.at[step, c], fin.at[step, c], leg2_recv.at[step, c]).wait()
            for k in range(blocks):
                row = c * half + k * BLK
                for j in range(blocks):
                    lines = []
                    for q in range(BLK // 16):
                        start = j * BLK + q * 16
                        lines.append(
                            fin[step, c, start // piece, pl.ds(start % piece, 16), pl.ds(k * BLK, BLK)]
                        )
                    block = jnp.concatenate(lines, axis=0).astype(jnp.float32)
                    mirror = jnp.transpose(block)
                    at = (pl.ds(row, BLK), pl.ds(j * BLK, BLK))
                    fresh = cur[at] - mirror * weight[at]
                    if step < STEPS - 1:
                        cur[at] = fresh
                        halo[step + 1, HOPS, pl.ds(row, BLK), pl.ds(j * BLK, BLK)] = fresh.astype(
                            jnp.bfloat16
                        )
                    else:
                        out_ref[at] = fresh
                if step < STEPS - 1:
                    start_own(step + 1, row // chunk_rows)

        def drain(d, carry):
            m = (own_place + d) % SPREAD
            leg2(step, m, 0).wait_send()
            leg2(step, m, 1).wait_send()
            return carry

        lax.fori_loop(1, SPREAD, drain, 0)
        leg2(step, own_place, 1 - core).wait_send()


def local(amplitudes, coupled_index, coupling_blocks, string_energy, shift_index):
    rows, cols = amplitudes.shape
    blocks = coupled_index.shape[0]
    couple = coupled_index.shape[1]
    half = rows // 2
    piece = half // SPREAD
    energy = string_energy.reshape(-1, BLK)
    any_space = pl.BlockSpec(memory_space=pl.ANY)
    vmem = pl.BlockSpec(memory_space=pltpu.VMEM)
    smem = pl.BlockSpec(memory_space=pltpu.SMEM)
    dma = pltpu.SemaphoreType.DMA
    return pl.pallas_call(
        kernel,
        out_shape=jax.ShapeDtypeStruct((rows, cols), jnp.float32),
        in_specs=[any_space, smem, any_space, vmem, smem],
        out_specs=vmem,
        scratch_shapes=[
            pltpu.VMEM((rows, cols), jnp.float32),
            pltpu.VMEM((STEPS, TILES, rows, cols), jnp.bfloat16),
            pltpu.VMEM((blocks + 1, couple, BLK, BLK), jnp.bfloat16),
            pltpu.VMEM((TILES, cols, cols), jnp.bfloat16),
            pltpu.VMEM((rows, cols), jnp.float32),
            pltpu.VMEM((STEPS, 2, SPREAD, piece, cols), jnp.bfloat16),
            pltpu.VMEM((STEPS, SPREAD, 2, piece, cols), jnp.bfloat16),
            pltpu.VMEM((STEPS, 2, SPREAD, piece, cols), jnp.bfloat16),
            pltpu.SMEM((blocks, couple), jnp.int32),
            dma((CHUNKS,)),
            dma,
            dma((STEPS, 6, CHUNKS)),
            dma((STEPS, 6, CHUNKS)),
            dma((STEPS, SPREAD)),
            dma((STEPS, SPREAD)),
            dma((STEPS, SPREAD, 2)),
            dma((STEPS, 2)),
        ],
        compiler_params=pltpu.CompilerParams(
            has_side_effects=True, vmem_limit_bytes=48 * 1024 * 1024
        ),
        cost_estimate=pl.CostEstimate(
            flops=2 * STEPS * TILES * rows * cols * cols, bytes_accessed=8 << 20, transcendentals=0
        ),
        name="residual_steps",
    )(amplitudes, coupled_index, coupling_blocks, energy, shift_index)


def solution(mesh):
    placed = (P("alpha", "beta"), P("beta", None), P("beta", None, None, None), P(), P())
    return jax.shard_map(
        local, mesh=mesh, in_specs=placed, out_specs=P("alpha", "beta"), check_vma=False
    )
```

time: 265 us -> 154 us (0.58)
  the two profiles are of different devices: /device:TPU:8 before, /device:TPU:5 now
where the time goes in v1:
time: 154 us; the launch traced here: 153 us
  Pallas kernels  147 us (95%)
  local copies, waits for them, and re-layouts  5.83 us (4%)
    pallas_call x1, Pallas kernels, local(): pl.pallas_call(kernel, out_shape=jax.ShapeDtypeStruct((rows, cols), jnp.f...  147 us
    unnamed x11, local copies, waits for them, and re-layouts  5.83 us

profile of v1, /device:TPU:5, one launch (start us, length us, event | category | flops | bytes accessed | tf_op | source)
XLA Modules:
  0.0 153.3 jit_solution(6010685044938470553)
XLA Ops:
  0.0 0.0 copy-start
  0.0 1.4 copy-done
  1.4 0.0 copy-start.1
  1.4 1.3 copy-done.1
  2.7 0.0 copy-start.2
  2.7 0.8 copy-done.2
  3.5 0.0 copy-start.3
  3.5 0.7 copy-done.3
  4.2 0.0 copy-start.4
  4.2 0.7 copy-done.4
  4.8 147.4 %residual_steps.1 = f32[768,384]{1,0:T(8,128)S(1)} custom-call(f32[768,384]{1,0:T(8,128)S(1)} %copy-done.1, s32[3,16]{1,0:T(4,128)S(1)} %copy-done.3, bf16[3,16,128,128]{3,2,1,0:T(8,128)(2,1)S(1)} %copy-done, f32[96,128]{1,0:T(8,128)S(1)} %bitcast.1, s32[2]{0:T(128)S(1)} %copy-done.4), custom_call_target="tpu_custom_call" | custom-call | flops 3170893824 | bytes 8388608 | tf_op jit(solution)/shard_map/residual_steps/pallas_call | solution.py:302
  152.2 1.0 copy.7
Async XLA Ops:
  0.0 1.4 copy-start
  1.4 1.3 copy-start.1
  2.7 0.8 copy-start.2
  3.5 0.7 copy-start.3
  4.2 0.7 copy-start.4

commit v2 on v1

--- a/solution.py
+++ b/solution.py
@@ -1,5 +1,3 @@
-import functools
-
 import jax
 import jax.numpy as jnp
 from jax import lax
@@ -15,6 +13,40 @@
 CHUNKS = 6
 SPREAD = 8
 MESH = pl.DeviceIdType.MESH
+ROUTES = (
+    (),
+    (64, 80, 192, 192, 1, 16, 17, 17),
+    (176, 89, 80, 122, 248, 24, 40, 40),
+    (168, 178, 128, 58, 240, 49, 48, 51),
+    (133, 192, 193, 193, 3, 4, 7, 67),
+    (146, 151, 211, 22, 16, 80, 80, 85),
+    (152, 152, 174, 232, 248, 248, 40, 56),
+    (88, 114, 128, 128, 199, 120, 48, 55),
+    (64, 64, 128, 128, 128, 192, 192, 200),
+    (30, 16, 1, 24, 64, 88, 128, 192),
+    (112, 144, 216, 233, 40, 104, 106, 170),
+    (255, 58, 64, 120, 131, 192, 192, 248),
+    (73, 74, 129, 142, 4, 5, 198, 202),
+    (168, 154, 222, 5, 192, 192, 216, 216),
+    (80, 184, 128, 208, 233, 6, 40, 198),
+    (186, 71, 120, 57, 56, 63, 192, 248),
+)
+
+
+def inbound_routes():
+    found = [[] for _ in ROUTES]
+    slots = {}
+    for piece in range(SPREAD):
+        for kind, row in enumerate(ROUTES):
+            if row:
+                at = kind ^ (row[piece] // 16) ^ (row[piece] % 16)
+                slots[kind, piece] = len(found[at])
+                found[at].append((row[piece], piece))
+    return found, slots
+
+
+INBOUND, SLOTS = inbound_routes()
+INSLOTS = max(len(entries) for entries in INBOUND)
 
 
 def kernel(
@@ -37,8 +69,6 @@
     left = 2 * ((chip + chips - 1) % chips)
     sibling = 2 * chip + 1 - core
     far = 2 * ((chip + chips + 2 * core - 1) % chips) + 1 - core
-    beta_group = beta // (2 * SPREAD)
-    own_place = chip % SPREAD
 
     def load(i):
         at = pl.ds(i * chunk_rows, chunk_rows)
@@ -50,6 +80,75 @@
     for i in range(CHUNKS):
         load(i).start()
     coup_copy().start()
+
+    def bits(value):
+        return [(value // 2**k) % 2 for k in range(4)]
+
+    alpha_bits, chip_bits = bits(alpha), bits(chip)
+    kind = sum((p + q) % 2 * 2**k for k, (p, q) in enumerate(zip(alpha_bits, chip_bits)))
+    stays = kind == 0
+
+    def pick(values):
+        chosen = jnp.int32(values[0])
+        for k in range(1, len(ROUTES)):
+            if values[k] != values[0]:
+                chosen = jnp.where(kind == k, values[k], chosen)
+        return chosen
+
+    def flipped(base, base_bits, flips):
+        for k in range(4):
+            base = base + (flips // 2**k) % 2 * (2**k * (1 - 2 * base_bits[k]))
+        return base
+
+    outs = []
+    back = []
+    for p in range(SPREAD):
+        route = pick([row[p] if row else 0 for row in ROUTES])
+        slot = pick([SLOTS.get((k, p), 0) for k in range(len(ROUTES))])
+        through = flipped(alpha, alpha_bits, route // 16)
+        outs.append((through, 2 * flipped(chip, chip_bits, route % 16) + core, slot))
+        back.append((flipped(chip, chip_bits, route // 16), flipped(alpha, alpha_bits, route % 16)))
+    ins = []
+    for n in range(INSLOTS):
+        entries = [row[n] if n < len(row) else (0, 0) for row in INBOUND]
+        counts = [n < len(row) for row in INBOUND]
+        valid = pick([int(v) for v in counts]) == 1
+        route = pick([v[0] for v in entries])
+        which = pick([v[1] for v in entries])
+        source_alpha = flipped(alpha, alpha_bits, route // 16)
+        source_chip = flipped(chip, chip_bits, route % 16)
+        home = jnp.logical_and(source_chip == alpha, source_alpha == chip)
+        ins.append((valid, which, source_chip, source_alpha, home))
+
+    barrier = pltpu.get_barrier_semaphore()
+
+    def greet(to_alpha, to_beta):
+        pl.semaphore_signal(
+            barrier, inc=1, device_id=(to_alpha, to_beta), device_id_type=MESH
+        )
+
+    for to_beta in (right + core, left + core, sibling, far):
+        greet(alpha, to_beta)
+    expected = jnp.int32(4)
+    for valid, _, to_alpha, to_chip, home in ins:
+
+        @pl.when(valid)
+        def _():
+            greet(to_chip, 2 * to_alpha + core)
+
+        expected = expected + jnp.where(valid, jnp.where(home, 1, 2), 0)
+
+    @pl.when(jnp.logical_not(stays))
+    def _():
+        for to_alpha, to_chip in back:
+            greet(to_alpha, 2 * to_chip + 1 - core)
+            same = jnp.logical_and(to_alpha == alpha, to_chip == chip)
+
+            @pl.when(jnp.logical_not(same))
+            def _():
+                greet(to_alpha, 2 * to_chip + core)
+
+    expected = expected + jnp.where(stays, 0, SPREAD)
 
     def remote(step, kind, i, src_slot, dst_slot, to):
         at = pl.ds(pl.multiple_of(i * chunk_rows, chunk_rows), chunk_rows)
@@ -91,6 +190,8 @@
         load(i).wait()
         at = pl.ds(i * chunk_rows, chunk_rows)
         halo[0, HOPS, at, :] = cur[at, :].astype(jnp.bfloat16)
+        if i == 0:
+            pl.semaphore_wait(barrier, expected)
         start_own(0, i)
 
     coup_copy().wait()
@@ -139,48 +240,51 @@
 
         lax.fori_loop(0, row_blocks, body, 0)
 
-    diagonal = (alpha == chip)
-
-    def leg1(step, i):
-        place = (own_place + i) % SPREAD
+    def leg1(step, p):
+        to_alpha, to_beta, slot = outs[p]
         return pltpu.make_async_remote_copy(
-            mixed.at[step, :, i],
-            inter.at[step, alpha % SPREAD],
-            leg1_send.at[step, i],
-            leg1_recv.at[step, alpha % SPREAD],
-            device_id=(chip, (alpha // SPREAD) * 2 * SPREAD + 2 * place + core),
+            mixed.at[step, :, p],
+            inter.at[step, slot],
+            leg1_send.at[step, p],
+            leg1_recv.at[step, slot],
+            device_id=(to_alpha, to_beta),
             device_id_type=MESH,
         )
 
-    def leg1_self(step):
+    def leg1_arrived(step, n):
         return pltpu.make_async_copy(
-            mixed.at[step, :, 0],
-            inter.at[step, alpha % SPREAD],
-            leg1_recv.at[step, alpha % SPREAD],
-        )
-
-    source_piece = (own_place + SPREAD - alpha % SPREAD) % SPREAD
-
-    def leg1_arrived(step, m):
+            inter.at[step, n], inter.at[step, n], leg1_recv.at[step, n]
+        )
+
+    def leg2(step, n, to_core):
+        _, which, to_alpha, to_chip, _ = ins[n]
+        return pltpu.make_async_remote_copy(
+            inter.at[step, n, to_core],
+            fin.at[step, core, which],
+            leg2_send.at[step, n, to_core],
+            leg2_recv.at[step, core],
+            device_id=(to_alpha, 2 * to_chip + to_core),
+            device_id_type=MESH,
+        )
+
+    def leg2_self(step, n):
         return pltpu.make_async_copy(
-            inter.at[step, m], inter.at[step, m], leg1_recv.at[step, m]
-        )
-
-    def leg2(step, m, to_core):
+            inter.at[step, n, core], fin.at[step, core, ins[n][1]], leg2_recv.at[step, core]
+        )
+
+    def leg0_sibling(step):
         return pltpu.make_async_remote_copy(
-            inter.at[step, m, to_core],
-            fin.at[step, core, source_piece],
-            leg2_send.at[step, m, to_core],
+            mixed.at[step, 1 - core],
+            fin.at[step, core],
+            leg1_send.at[step, 0],
             leg2_recv.at[step, core],
-            device_id=(alpha, beta_group * 2 * SPREAD + 2 * m + to_core),
+            device_id=(alpha, sibling),
             device_id_type=MESH,
         )
 
-    def leg2_self(step):
+    def leg0_self(step):
         return pltpu.make_async_copy(
-            inter.at[step, own_place, core],
-            fin.at[step, core, source_piece],
-            leg2_recv.at[step, core],
+            mixed.at[step, core], fin.at[step, core], leg2_recv.at[step, core]
         )
 
     for step in range(STEPS):
@@ -196,8 +300,6 @@
             return carry
 
         lax.fori_loop(0, CHUNKS, forward, 0)
-
-        pieces_per_chunk = chunk_rows // piece if chunk_rows >= piece else 1
 
         def mix(i, carry):
             for copy in halo_kinds[2:]:
@@ -224,33 +326,35 @@
 
         lax.fori_loop(0, CHUNKS, mix, 0)
 
-        for i in range(SPREAD):
-            if i == 0:
-                pl.when(diagonal)(leg1_self(step).start)
-                pl.when(jnp.logical_not(diagonal))(leg1(step, i).start)
-            else:
-                leg1(step, i).start()
-
-        def onward(d, carry):
-            m = (own_place + d) % SPREAD
-            leg1_arrived(step, m).wait()
-            leg2(step, m, 0).start()
-            leg2(step, m, 1).start()
-            return carry
-
-        lax.fori_loop(1, SPREAD, onward, 0)
-        leg1_arrived(step, own_place).wait()
-        leg2(step, own_place, 1 - core).start()
-        leg2_self(step).start()
+        @pl.when(stays)
+        def _():
+            leg0_sibling(step).start()
+            leg0_self(step).start()
+
+        @pl.when(jnp.logical_not(stays))
+        def _():
+            for p in range(SPREAD):
+                leg1(step, p).start()
+
+        for n in range(INSLOTS):
+            valid, home = ins[n][0], ins[n][4]
+
+            @pl.when(valid)
+            def _():
+                leg1_arrived(step, n).wait()
+                leg2(step, n, 1 - core).start()
+                pl.when(home)(leg2_self(step, n).start)
+                pl.when(jnp.logical_not(home))(leg2(step, n, core).start)
 
         for copy in halo_kinds:
             for i in range(CHUNKS):
                 copy(step, i).wait_send()
-        for i in range(SPREAD):
-            if i == 0:
-                pl.when(jnp.logical_not(diagonal))(leg1(step, i).wait_send)
-            else:
-                leg1(step, i).wait_send()
+        pl.when(stays)(leg0_sibling(step).wait_send)
+
+        @pl.when(jnp.logical_not(stays))
+        def _():
+            for p in range(SPREAD):
+                leg1(step, p).wait_send()
 
         per_half = CHUNKS // 2
         for c in range(2):
@@ -278,14 +382,13 @@
                 if step < STEPS - 1:
                     start_own(step + 1, row // chunk_rows)
 
-        def drain(d, carry):
-            m = (own_place + d) % SPREAD
-            leg2(step, m, 0).wait_send()
-            leg2(step, m, 1).wait_send()
-            return carry
-
-        lax.fori_loop(1, SPREAD, drain, 0)
-        leg2(step, own_place, 1 - core).wait_send()
+        for n in range(INSLOTS):
+            valid, home = ins[n][0], ins[n][4]
+
+            @pl.when(valid)
+            def _():
+                leg2(step, n, 1 - core).wait_send()
+                pl.when(jnp.logical_not(home))(leg2(step, n, core).wait_send)
 
 
 def local(amplitudes, coupled_index, coupling_blocks, string_energy, shift_index):
@@ -295,14 +398,14 @@
     half = rows // 2
     piece = half // SPREAD
     energy = string_energy.reshape(-1, BLK)
-    any_space = pl.BlockSpec(memory_space=pl.ANY)
+    in_hbm = pl.BlockSpec(memory_space=pltpu.HBM)
     vmem = pl.BlockSpec(memory_space=pltpu.VMEM)
     smem = pl.BlockSpec(memory_space=pltpu.SMEM)
     dma = pltpu.SemaphoreType.DMA
     return pl.pallas_call(
         kernel,
         out_shape=jax.ShapeDtypeStruct((rows, cols), jnp.float32),
-        in_specs=[any_space, smem, any_space, vmem, smem],
+        in_specs=[in_hbm, smem, in_hbm, vmem, smem],
         out_specs=vmem,
         scratch_shapes=[
             pltpu.VMEM((rows, cols), jnp.float32),
@@ -311,7 +414,7 @@
             pltpu.VMEM((TILES, cols, cols), jnp.bfloat16),
             pltpu.VMEM((rows, cols), jnp.float32),
             pltpu.VMEM((STEPS, 2, SPREAD, piece, cols), jnp.bfloat16),
-            pltpu.VMEM((STEPS, SPREAD, 2, piece, cols), jnp.bfloat16),
+            pltpu.VMEM((STEPS, INSLOTS, 2, piece, cols), jnp.bfloat16),
             pltpu.VMEM((STEPS, 2, SPREAD, piece, cols), jnp.bfloat16),
             pltpu.SMEM((blocks, couple), jnp.int32),
             dma((CHUNKS,)),
@@ -319,12 +422,12 @@
             dma((STEPS, 6, CHUNKS)),
             dma((STEPS, 6, CHUNKS)),
             dma((STEPS, SPREAD)),
-            dma((STEPS, SPREAD)),
-            dma((STEPS, SPREAD, 2)),
+            dma((STEPS, INSLOTS)),
+            dma((STEPS, INSLOTS, 2)),
             dma((STEPS, 2)),
         ],
         compiler_params=pltpu.CompilerParams(
-            has_side_effects=True, vmem_limit_bytes=48 * 1024 * 1024
+            collective_id=0, has_side_effects=True, vmem_limit_bytes=62 * 1024 * 1024
         ),
         cost_estimate=pl.CostEstimate(
             flops=2 * STEPS * TILES * rows * cols * cols, bytes_accessed=8 << 20, transcendentals=0

time: 154 us -> 117 us (0.76)
  the two profiles are of different devices: /device:TPU:5 before, /device:TPU:8 now
where the time goes in v2:
time: 117 us
  Pallas kernels  114 us (97%)
  local copies, waits for them, and re-layouts  2.36 us (2%)
    pallas_call x1, Pallas kernels, local(): pl.pallas_call(kernel, out_shape=jax.ShapeDtypeStruct((rows, cols), jnp.f...  114 us
    unnamed x1, local copies, waits for them, and re-layouts  2.36 us

profile of v2, /device:TPU:8, one launch (start us, length us, event | category | flops | bytes accessed | tf_op | source)
XLA Modules:
  0.0 116.5 jit_solution(5372122731081913846)
XLA Ops:
  0.0 114.1 %residual_steps.1 = f32[768,384]{1,0:T(8,128)} custom-call(f32[768,384]{1,0:T(8,128)} %amp_hbm.1, s32[3,16]{1,0:T(4,128)} %idx_ref.1, bf16[3,16,128,128]{3,2,1,0:T(8,128)(2,1)} %coup_hbm.1, f32[96,128]{1,0:T(8,128)} %bitcast.1, s32[2]{0:T(128)} %shift_ref.1), custom_call_target="tpu_custom_call" | custom-call | flops 3170893824 | bytes 8388608 | tf_op jit(solution)/shard_map/residual_steps/pallas_call | solution.py:405
  114.1 2.4 %copy.7 = f32[768,384]{1,0:T(8,128)} copy(f32[768,384]{1,0:T(8,128)} %residual_steps.1) | data formatting | bytes 2359296

commit v3 on v2

--- a/solution.py
+++ b/solution.py
@@ -12,52 +12,60 @@
 TILES = 2 * HOPS + 1
 CHUNKS = 6
 SPREAD = 8
+GROUPS = 4
+LEGWIN = 4
 MESH = pl.DeviceIdType.MESH
 ROUTES = (
     (),
-    (64, 80, 192, 192, 1, 16, 17, 17),
-    (176, 89, 80, 122, 248, 24, 40, 40),
-    (168, 178, 128, 58, 240, 49, 48, 51),
-    (133, 192, 193, 193, 3, 4, 7, 67),
-    (146, 151, 211, 22, 16, 80, 80, 85),
-    (152, 152, 174, 232, 248, 248, 40, 56),
-    (88, 114, 128, 128, 199, 120, 48, 55),
-    (64, 64, 128, 128, 128, 192, 192, 200),
-    (30, 16, 1, 24, 64, 88, 128, 192),
-    (112, 144, 216, 233, 40, 104, 106, 170),
-    (255, 58, 64, 120, 131, 192, 192, 248),
-    (73, 74, 129, 142, 4, 5, 198, 202),
-    (168, 154, 222, 5, 192, 192, 216, 216),
-    (80, 184, 128, 208, 233, 6, 40, 198),
-    (186, 71, 120, 57, 56, 63, 192, 248),
+    (217, 129, 193, 64, 16, 208, 24, 211),
+    (40, 217, 238, 120, 88, 144, 170, 48),
+    (248, 104, 187, 114, 48, 51, 128, 216),
+    (64, 194, 7, 65, 133, 71, 131, 193),
+    (40, 151, 144, 21, 42, 21, 210, 80),
+    (184, 144, 254, 56, 232, 72, 24, 120),
+    (240, 246, 48, 104, 64, 120, 55, 246),
+    (64, 192, 128, 64, 64, 192, 128, 8),
+    (216, 128, 88, 1, 193, 128, 64, 192),
+    (40, 192, 40, 238, 111, 120, 144, 109),
+    (64, 58, 184, 195, 3, 168, 120, 249),
+    (135, 216, 75, 5, 10, 137, 4, 129),
+    (24, 90, 158, 221, 5, 94, 24, 216),
+    (187, 104, 216, 144, 41, 216, 184, 46),
+    (128, 63, 171, 7, 128, 190, 56, 192),
 )
 
 
 def inbound_routes():
-    found = [[] for _ in ROUTES]
+    groups = []
     slots = {}
-    for piece in range(SPREAD):
-        for kind, row in enumerate(ROUTES):
-            if row:
-                at = kind ^ (row[piece] // 16) ^ (row[piece] % 16)
-                slots[kind, piece] = len(found[at])
-                found[at].append((row[piece], piece))
-    return found, slots
-
-
-INBOUND, SLOTS = inbound_routes()
-INSLOTS = max(len(entries) for entries in INBOUND)
+    base = 0
+    for group in range(GROUPS):
+        found = [[] for _ in ROUTES]
+        for piece in range(group * SPREAD // GROUPS, (group + 1) * SPREAD // GROUPS):
+            for kind, row in enumerate(ROUTES):
+                if row:
+                    at = kind ^ (row[piece] // 16) ^ (row[piece] % 16)
+                    slots[kind, piece] = base + len(found[at])
+                    found[at].append((row[piece], piece))
+        width = max(len(entries) for entries in found)
+        groups.append((base, width, found))
+        base += width
+    return groups, slots, base
+
+
+INBOUND, SLOTS, INSLOTS = inbound_routes()
 
 
 def kernel(
     amp_hbm, idx_ref, coup_hbm, energy_ref, shift_ref, out_ref,
-    cur, halo, coup, banded, weight, mixed, inter, fin, pos_ref,
+    cur, halo, coup, banded, weight, mixed, inter, fin, partial, pos_ref,
     load_sem, coup_sem, hsend, hrecv, leg1_send, leg1_recv, leg2_send, leg2_recv,
 ):
     rows, cols = amp_hbm.shape
     chunk_rows = rows // CHUNKS
     half = rows // 2
     piece = half // SPREAD
+    per_group = SPREAD // GROUPS
     blocks = cols // BLK
     couple = coup_hbm.shape[1]
     alpha = lax.axis_index("alpha")
@@ -65,10 +73,11 @@
     chip = beta // 2
     core = beta % 2
     chips = lax.axis_size("beta") // 2
-    right = 2 * ((chip + 1) % chips)
-    left = 2 * ((chip + chips - 1) % chips)
+    next_chip = (chip + chips + 2 * core - 1) % chips
+    ahead = 2 * next_chip + core
+    behind = 2 * ((chip + chips + 1 - 2 * core) % chips) + core
     sibling = 2 * chip + 1 - core
-    far = 2 * ((chip + chips + 2 * core - 1) % chips) + 1 - core
+    far = 2 * next_chip + 1 - core
 
     def load(i):
         at = pl.ds(i * chunk_rows, chunk_rows)
@@ -109,10 +118,9 @@
         outs.append((through, 2 * flipped(chip, chip_bits, route % 16) + core, slot))
         back.append((flipped(chip, chip_bits, route // 16), flipped(alpha, alpha_bits, route % 16)))
     ins = []
-    for n in range(INSLOTS):
-        entries = [row[n] if n < len(row) else (0, 0) for row in INBOUND]
-        counts = [n < len(row) for row in INBOUND]
-        valid = pick([int(v) for v in counts]) == 1
+    for found, n in [(found, n) for _, width, found in INBOUND for n in range(width)]:
+        entries = [row[n] if n < len(row) else (0, 0) for row in found]
+        valid = pick([int(n < len(row)) for row in found]) == 1
         route = pick([v[0] for v in entries])
         which = pick([v[1] for v in entries])
         source_alpha = flipped(alpha, alpha_bits, route // 16)
@@ -127,7 +135,7 @@
             barrier, inc=1, device_id=(to_alpha, to_beta), device_id_type=MESH
         )
 
-    for to_beta in (right + core, left + core, sibling, far):
+    for to_beta in (ahead, behind, sibling, far):
         greet(alpha, to_beta)
     expected = jnp.int32(4)
     for valid, _, to_alpha, to_chip, home in ins:
@@ -161,29 +169,29 @@
             device_id_type=MESH,
         )
 
-    def to_right(step, i):
-        return remote(step, 0, i, 3, 1, right + core)
-
-    def to_left(step, i):
-        return remote(step, 1, i, 3, 5, left + core)
+    def lead(step, i):
+        return remote(step, 0, i, 3, 5 - 4 * core, ahead)
+
+    def trail(step, i):
+        return remote(step, 1, i, 3, 1 + 4 * core, behind)
 
     def to_sibling(step, i):
         return remote(step, 2, i, 3, 2 * core + 2, sibling)
 
-    def pass_left_tile(step, i):
-        return remote(step, 3, i, 1, 2 * core, sibling)
-
-    def pass_right_tile(step, i):
-        return remote(step, 4, i, 5, 2 * core + 4, sibling)
+    def pass_lead(step, i):
+        return remote(step, 3, i, 5 - 4 * core, 4 - 2 * core, sibling)
+
+    def pass_trail(step, i):
+        return remote(step, 4, i, 1 + 4 * core, 6 * core, sibling)
 
     def pass_far(step, i):
         return remote(step, 5, i, 5 - 4 * core, 6 - 6 * core, far)
 
-    halo_kinds = (to_right, to_left, to_sibling, pass_left_tile, pass_right_tile, pass_far)
+    halo_kinds = (lead, trail, to_sibling, pass_lead, pass_trail, pass_far)
 
     def start_own(step, i):
-        to_right(step, i).start()
-        to_left(step, i).start()
+        lead(step, i).start()
+        trail(step, i).start()
         to_sibling(step, i).start()
 
     for i in range(CHUNKS):
@@ -292,24 +300,43 @@
         fill_weight(step, shift)
 
         def forward(i, carry):
-            to_right(step, i).wait_recv()
-            pass_left_tile(step, i).start()
-            to_left(step, i).wait_recv()
-            pass_right_tile(step, i).start()
+            lead(step, i).wait_recv()
             pass_far(step, i).start()
+            pass_lead(step, i).start()
             return carry
 
         lax.fori_loop(0, CHUNKS, forward, 0)
 
-        def mix(i, carry):
-            for copy in halo_kinds[2:]:
+        def share(i, carry):
+            trail(step, i).wait_recv()
+            pass_trail(step, i).start()
+            return carry
+
+        lax.fori_loop(0, CHUNKS, share, 0)
+
+        def gather(i, carry):
+            for copy in halo_kinds[2:5]:
                 copy(step, i).wait_recv()
             at = pl.ds(pl.multiple_of(i * chunk_rows, chunk_rows), chunk_rows)
-            acc = jnp.dot(halo[step, 0, at, :], banded[0], preferred_element_type=jnp.float32)
-            for slot in range(1, TILES):
-                acc = acc + jnp.dot(
+            acc = None
+            for near in range(TILES - 1):
+                slot = near + 1 - core
+                part = jnp.dot(
                     halo[step, slot, at, :], banded[slot], preferred_element_type=jnp.float32
                 )
+                acc = part if acc is None else acc + part
+            partial[at, :] = acc
+            return carry
+
+        lax.fori_loop(0, CHUNKS, gather, 0)
+
+        def mix(i, carry):
+            pass_far(step, i).wait_recv()
+            at = pl.ds(pl.multiple_of(i * chunk_rows, chunk_rows), chunk_rows)
+            slot = (TILES - 1) * core
+            acc = partial[at, :] + jnp.dot(
+                halo[step, slot, at, :], banded[slot], preferred_element_type=jnp.float32
+            )
             low = acc.astype(jnp.bfloat16)
             per_half = CHUNKS // 2
             flat = mixed.at[step, i // per_half]
@@ -319,32 +346,49 @@
                 flat[start // piece, pl.ds(pl.multiple_of(start % piece, 16), 16), :] = low[
                     q * 16 : (q + 1) * 16
                 ]
-            wide = low.astype(jnp.float32)
+            partial[at, :] = low.astype(jnp.float32)
+            return carry
+
+        lax.fori_loop(0, CHUNKS, mix, 0)
+
+        def rebase(i, carry):
+            at = pl.ds(pl.multiple_of(i * chunk_rows, chunk_rows), chunk_rows)
             factor = weight[at, :]
-            cur[at, :] = cur[at, :] * (1.0 + shift * factor) - wide * factor
-            return carry
-
-        lax.fori_loop(0, CHUNKS, mix, 0)
+            cur[at, :] = cur[at, :] * (1.0 + shift * factor) - partial[at, :] * factor
+            return carry
+
+        def outward(g):
+            @pl.when(jnp.logical_not(stays))
+            def _():
+                for p in range(g * per_group, (g + 1) * per_group):
+                    leg1(step, p).start()
+
+        def onward(g):
+            base, width, _ = INBOUND[g]
+            for n in range(base, base + width):
+                valid, home = ins[n][0], ins[n][4]
+
+                @pl.when(valid)
+                def _():
+                    leg1_arrived(step, n).wait()
+                    leg2(step, n, 1 - core).start()
+                    pl.when(home)(leg2_self(step, n).start)
+                    pl.when(jnp.logical_not(home))(leg2(step, n, core).start)
+
+        for g in range(LEGWIN):
+            outward(g)
 
         @pl.when(stays)
         def _():
             leg0_sibling(step).start()
             leg0_self(step).start()
 
-        @pl.when(jnp.logical_not(stays))
-        def _():
-            for p in range(SPREAD):
-                leg1(step, p).start()
-
-        for n in range(INSLOTS):
-            valid, home = ins[n][0], ins[n][4]
-
-            @pl.when(valid)
-            def _():
-                leg1_arrived(step, n).wait()
-                leg2(step, n, 1 - core).start()
-                pl.when(home)(leg2_self(step, n).start)
-                pl.when(jnp.logical_not(home))(leg2(step, n, core).start)
+        lax.fori_loop(0, CHUNKS, rebase, 0)
+
+        for g in range(GROUPS):
+            onward(g)
+            if g + LEGWIN < GROUPS:
+                outward(g + LEGWIN)
 
         for copy in halo_kinds:
             for i in range(CHUNKS):
@@ -416,6 +460,7 @@
             pltpu.VMEM((STEPS, 2, SPREAD, piece, cols), jnp.bfloat16),
             pltpu.VMEM((STEPS, INSLOTS, 2, piece, cols), jnp.bfloat16),
             pltpu.VMEM((STEPS, 2, SPREAD, piece, cols), jnp.bfloat16),
+            pltpu.VMEM((rows, cols), jnp.float32),
             pltpu.SMEM((blocks, couple), jnp.int32),
             dma((CHUNKS,)),
             dma,

time: 117 us -> 114 us (0.974)
  the two profiles are of different devices: /device:TPU:8 before, /device:TPU:109 now
where the time goes in v3:
time: 114 us
  Pallas kernels  111 us (97%)
  local copies, waits for them, and re-layouts  2.36 us (2%)
    pallas_call x1, Pallas kernels, local(): pl.pallas_call(kernel, out_shape=jax.ShapeDtypeStruct((rows, cols), jnp.f...  111 us
    unnamed x1, local copies, waits for them, and re-layouts  2.36 us

profile of v3, /device:TPU:109, one launch (start us, length us, event | category | flops | bytes accessed | tf_op | source)
XLA Modules:
  0.0 113.9 jit_solution(11746971719741411333)
XLA Ops:
  0.0 111.5 %residual_steps.1 = f32[768,384]{1,0:T(8,128)} custom-call(f32[768,384]{1,0:T(8,128)} %amp_hbm.1, s32[3,16]{1,0:T(4,128)} %idx_ref.1, bf16[3,16,128,128]{3,2,1,0:T(8,128)(2,1)} %coup_hbm.1, f32[96,128]{1,0:T(8,128)} %bitcast.1, s32[2]{0:T(128)} %shift_ref.1), custom_call_target="tpu_custom_call" | custom-call | flops 3170893824 | bytes 8388608 | tf_op jit(solution)/shard_map/residual_steps/pallas_call | solution.py:449
  111.5 2.4 %copy.7 = f32[768,384]{1,0:T(8,128)} copy(f32[768,384]{1,0:T(8,128)} %residual_steps.1) | data formatting | bytes 2359296

commit v4 on v3

--- a/solution.py
+++ b/solution.py
@@ -59,7 +59,7 @@
 def kernel(
     amp_hbm, idx_ref, coup_hbm, energy_ref, shift_ref, out_ref,
     cur, halo, coup, banded, weight, mixed, inter, fin, partial, pos_ref,
-    load_sem, coup_sem, hsend, hrecv, leg1_send, leg1_recv, leg2_send, leg2_recv,
+    load_sem, store_sem, coup_sem, hsend, hrecv, leg1_send, leg1_recv, leg2_send, leg2_recv,
 ):
     rows, cols = amp_hbm.shape
     chunk_rows = rows // CHUNKS
@@ -83,6 +83,10 @@
         at = pl.ds(i * chunk_rows, chunk_rows)
         return pltpu.make_async_copy(amp_hbm.at[at], cur.at[at], load_sem.at[i])
 
+    def store(k):
+        at = pl.ds(k * BLK, BLK)
+        return pltpu.make_async_copy(cur.at[at], out_ref.at[at], store_sem.at[k])
+
     def coup_copy():
         return pltpu.make_async_copy(coup_hbm, coup.at[pl.ds(0, blocks)], coup_sem)
 
@@ -416,15 +420,15 @@
                     mirror = jnp.transpose(block)
                     at = (pl.ds(row, BLK), pl.ds(j * BLK, BLK))
                     fresh = cur[at] - mirror * weight[at]
+                    cur[at] = fresh
                     if step < STEPS - 1:
-                        cur[at] = fresh
                         halo[step + 1, HOPS, pl.ds(row, BLK), pl.ds(j * BLK, BLK)] = fresh.astype(
                             jnp.bfloat16
                         )
-                    else:
-                        out_ref[at] = fresh
                 if step < STEPS - 1:
                     start_own(step + 1, row // chunk_rows)
+                else:
+                    store(row // BLK).start()
 
         for n in range(INSLOTS):
             valid, home = ins[n][0], ins[n][4]
@@ -433,6 +437,9 @@
             def _():
                 leg2(step, n, 1 - core).wait_send()
                 pl.when(jnp.logical_not(home))(leg2(step, n, core).wait_send)
+
+    for k in range(row_blocks):
+        store(k).wait()
 
 
 def local(amplitudes, coupled_index, coupling_blocks, string_energy, shift_index):
@@ -450,7 +457,7 @@
         kernel,
         out_shape=jax.ShapeDtypeStruct((rows, cols), jnp.float32),
         in_specs=[in_hbm, smem, in_hbm, vmem, smem],
-        out_specs=vmem,
+        out_specs=in_hbm,
         scratch_shapes=[
             pltpu.VMEM((rows, cols), jnp.float32),
             pltpu.VMEM((STEPS, TILES, rows, cols), jnp.bfloat16),
@@ -463,6 +470,7 @@
             pltpu.VMEM((rows, cols), jnp.float32),
             pltpu.SMEM((blocks, couple), jnp.int32),
             dma((CHUNKS,)),
+            dma((rows // BLK,)),
             dma,
             dma((STEPS, 6, CHUNKS)),
             dma((STEPS, 6, CHUNKS)),

time: 114 us -> 114 us (level)
  no operation moved by 1% of the time
where the time goes in v4:
time: 114 us
  Pallas kernels  111 us (97%)
  local copies, waits for them, and re-layouts  2.36 us (2%)
    pallas_call x1, Pallas kernels, local(): pl.pallas_call(kernel, out_shape=jax.ShapeDtypeStruct((rows, cols), jnp.f...  111 us
    unnamed x1, local copies, waits for them, and re-layouts  2.36 us

profile of v4, /device:TPU:109, one launch (start us, length us, event | category | flops | bytes accessed | tf_op | source)
XLA Modules:
  0.0 113.5 jit_solution(15879316985520859425)
XLA Ops:
  0.0 111.2 %residual_steps.1 = f32[768,384]{1,0:T(8,128)} custom-call(f32[768,384]{1,0:T(8,128)} %amp_hbm.1, s32[3,16]{1,0:T(4,128)} %idx_ref.1, bf16[3,16,128,128]{3,2,1,0:T(8,128)(2,1)} %coup_hbm.1, f32[96,128]{1,0:T(8,128)} %bitcast.1, s32[2]{0:T(128)} %shift_ref.1), custom_call_target="tpu_custom_call" | custom-call | flops 3170893824 | bytes 8388608 | tf_op jit(solution)/shard_map/residual_steps/pallas_call | solution.py:456
  111.2 2.4 %copy.7 = f32[768,384]{1,0:T(8,128)} copy(f32[768,384]{1,0:T(8,128)} %residual_steps.1) | data formatting | bytes 2359296
